TPU v7x, 512 devices: a whole 4x4x16 slice. The times are simulated.
512 devices in a mesh: seq: 64 (over z, y_lo, core), head: 8 (over x, y_hi).
Axes of the slice: x: 4, y: 4 (y_hi: 2, y_lo: 2; y = y_hi * 2 + y_lo), z: 16, core: 2. Of those that a mesh axis runs over, the one named last changes fastest.
Arguments:
- queries: bfloat16 [4096, 3072], P('seq', 'head'), may hold values from -10 to 10
- suffix_latent: bfloat16 [4096, 576], P('seq'), may hold values from -6 to 6
- prefix_latent: bfloat16 [1024, 576], P('seq'), may hold values from -6 to 6
- kv_up: bfloat16 [16, 512, 256], P('head'), may hold values from -0.25 to 0.25
- w_out: bfloat16 [2048, 2048], P('head'), may hold values from -2 to 2
- residual: bfloat16 [4096, 2048], P('seq'), may hold values from -400 to 400
- norm_gain: bfloat16 [2048], replicated, may hold values from 0.099609375 to 1.8984375
- router: bfloat16 [2048, 64], replicated, may hold values from -0.125 to 0.125
- w_gate: bfloat16 [64, 2048, 1408], P('seq', None, 'head'), may hold values from -0.125 to 0.125
- w_up: bfloat16 [64, 2048, 1408], P('seq', None, 'head'), may hold values from -0.125 to 0.125
- w_down: bfloat16 [64, 1408, 2048], P('seq', 'head'), may hold values from -0.15625 to 0.15625
- lengths: int32 [128], replicated, may hold values from 1 to 64, 4096 in all
- group_map: int32 [128], replicated, may hold values from 0 to 1
- expert_ids: int32 [4096, 6], P('seq'), may hold values from 0 to 63, all different within a row; in each aligned block of 64 rows (0 to 63, 64 to 127, ...) at most 9 rows name the same one
Outputs:
- attention: bfloat16 [4096, 2048], P('seq', 'head')
- expert_out: bfloat16 [4096, 2048], P('seq', 'head')
Inputs may be any that keep to these rules, and one draw needn't show every extreme that they name: `lengths`: the requests cover the 4096 tokens exactly; each has 1 to 64 tokens, and one has exactly 64. `expert_ids`: each token names 6 different experts. Among the 64 tokens of one index of seq (aligned blocks of rows) no expert is named more than 9 times, a bound that some block reaches.
All inputs are finite; a program needn't handle non-finite values.
Results may differ from a plain program's by a relative error of at most 0.027.
Values may be sent and summed in bfloat16 or wider, within the bound.
A program may use at most 64 MiB of HBM per device.

v0:
```python
import math

import jax
import jax.numpy as jnp
from jax import lax
from jax.sharding import PartitionSpec as P

D = 2048
NOPE = 128
ROPE = 64
VDIM = 128
LAT = 512
TOPK = 6
PRE_LEN = 512


score_scale = 1.0 / math.sqrt(192.0)
route_scale = 2.446
norm_eps = 1e-06


def shifted(value, axis, by):
    peers = lax.axis_size(axis)
    pairs = [(i, i + by) for i in range(peers) if 0 <= i + by < peers]
    return lax.ppermute(value, axis, pairs)


def request_info(lengths, group_map, position):
    request_ends = jnp.cumsum(lengths)
    request_starts = request_ends - lengths
    request_index = jnp.sum((request_ends[None, :] <= position[:, None]).astype(jnp.int32), axis=1)
    member = (
        request_index[:, None] == jnp.arange(lengths.shape[0], dtype=jnp.int32)[None, :]
    ).astype(jnp.int32)
    first_token = jnp.sum(member * request_starts[None, :], axis=1)
    token_group = jnp.sum(member * group_map[None, :], axis=1)
    return (first_token, token_group)


def on_device(
    queries,
    suffix_latent,
    prefix_latent,
    kv_up,
    w_out,
    residual,
    norm_gain,
    router,
    w_gate,
    w_up,
    w_down,
    lengths,
    group_map,
    expert_ids,
):
    tok_count = queries.shape[0]
    head_local = kv_up.shape[0]
    seq_index = lax.axis_index("seq")
    first_row = seq_index * tok_count
    position = first_row + jnp.arange(tok_count, dtype=jnp.int32)
    first_token, token_group = request_info(lengths, group_map, position)
    query_block = queries.reshape(tok_count, head_local, NOPE + ROPE)
    absorbed = jnp.einsum(
        "thn,hln->thl",
        query_block[:, :, :NOPE],
        kv_up[:, :, :NOPE],
        preferred_element_type=jnp.float32,
    ).astype(jnp.bfloat16)
    joined = jnp.concatenate([absorbed, query_block[:, :, NOPE:]], axis=2).reshape(
        tok_count * head_local, LAT + ROPE
    )
    earlier = shifted(suffix_latent, "seq", 1)
    nearby = jnp.concatenate([earlier, suffix_latent], axis=0)
    near_pos = first_row - tok_count + jnp.arange(2 * tok_count, dtype=jnp.int32)
    near_seen = (near_pos[None, :] >= first_token[:, None]) & (
        near_pos[None, :] <= position[:, None]
    )
    near_seen = jnp.repeat(near_seen, head_local, axis=0)
    scores = jnp.dot(joined, nearby.T, preferred_element_type=jnp.float32) * score_scale
    row_max = jnp.max(jnp.where(near_seen, scores, -jnp.inf), axis=1, keepdims=True)
    weights = jnp.where(near_seen, jnp.exp(scores - row_max), 0.0)
    total = jnp.sum(weights, axis=1, keepdims=True)
    weighted = jnp.dot(
        weights.astype(jnp.bfloat16), nearby[:, :LAT], preferred_element_type=jnp.float32
    )
    group_rows = jnp.repeat(token_group, head_local)
    piece = lax.all_gather(prefix_latent, "seq", axis=0, tiled=True)
    row_group = jnp.arange(piece.shape[0], dtype=jnp.int32) // PRE_LEN
    visible = row_group[None, :] == group_rows[:, None]
    piece_scores = jnp.dot(joined, piece.T, preferred_element_type=jnp.float32) * score_scale
    new_max = jnp.maximum(
        row_max, jnp.max(jnp.where(visible, piece_scores, -jnp.inf), axis=1, keepdims=True)
    )
    piece_weights = jnp.where(visible, jnp.exp(piece_scores - new_max), 0.0)
    factor = jnp.exp(row_max - new_max)
    new_total = total * factor + jnp.sum(piece_weights, axis=1, keepdims=True)
    new_weighted = weighted * factor + jnp.dot(
        piece_weights.astype(jnp.bfloat16), piece[:, :LAT], preferred_element_type=jnp.float32
    )
    mixed = (new_weighted / new_total).astype(jnp.bfloat16).reshape(tok_count, head_local, LAT)
    heads_out = jnp.einsum(
        "thl,hlv->thv", mixed, kv_up[:, :, NOPE:], preferred_element_type=jnp.float32
    ).astype(jnp.bfloat16)
    partial_value = jnp.dot(
        heads_out.reshape(tok_count, head_local * VDIM), w_out, preferred_element_type=jnp.float32
    )
    col_width = D // lax.axis_size("head")
    col_start = lax.axis_index("head") * col_width
    attention_sum = lax.psum(partial_value.astype(jnp.bfloat16), "head").astype(jnp.float32)
    attention = lax.dynamic_slice_in_dim(attention_sum, col_start, col_width, 1).astype(
        jnp.bfloat16
    )
    hidden_state = residual.astype(jnp.float32) + attention_sum
    mean_square = jnp.mean(hidden_state * hidden_state, axis=1, keepdims=True)
    normed = (
        hidden_state * lax.rsqrt(mean_square + norm_eps) * norm_gain.astype(jnp.float32)
    ).astype(jnp.bfloat16)
    logits = jnp.dot(normed, router, preferred_element_type=jnp.float32)
    expert_count = router.shape[1]
    capacity = (3 * tok_count * TOPK + 2 * expert_count - 1) // (2 * expert_count)
    member = expert_ids[:, :, None] == jnp.arange(expert_count, dtype=jnp.int32)[None, None, :]
    chosen = jnp.sum(jnp.where(member, jax.nn.sigmoid(logits)[:, None, :], 0.0), axis=2)
    gates = chosen / jnp.sum(chosen, axis=1, keepdims=True) * route_scale
    flat_member = member.reshape(tok_count * TOPK, expert_count).astype(jnp.int32)
    running = jnp.cumsum(flat_member, axis=0)
    slot_rank = jnp.sum(flat_member * running, axis=1) - 1
    slot_index = expert_ids.reshape(-1) * capacity + slot_rank
    pair_token = jnp.arange(tok_count * TOPK, dtype=jnp.int32) // TOPK
    source_row = jnp.zeros((expert_count * capacity,), jnp.int32).at[slot_index].set(pair_token + 1)
    padded_rows = jnp.concatenate([jnp.zeros((1, normed.shape[1]), jnp.bfloat16), normed], axis=0)
    outgoing = padded_rows[source_row].reshape(expert_count, capacity, normed.shape[1])
    local_experts = w_gate.shape[0]
    received = lax.all_to_all(outgoing, "seq", split_axis=0, concat_axis=0, tiled=True)
    shaped = received.reshape(-1, local_experts, received.shape[1], received.shape[2])
    gate_part = jnp.einsum("secd,edf->secf", shaped, w_gate, preferred_element_type=jnp.float32)
    up_part = jnp.einsum("secd,edf->secf", shaped, w_up, preferred_element_type=jnp.float32)
    inner = (jax.nn.silu(gate_part) * up_part).astype(jnp.bfloat16)
    down_part = jnp.einsum(
        "secf,efd->secd", inner, w_down, preferred_element_type=jnp.float32
    ).astype(jnp.bfloat16)
    produced = down_part.reshape(-1, down_part.shape[2], down_part.shape[3])
    returned = lax.all_to_all(produced, "seq", split_axis=0, concat_axis=0, tiled=True)
    picked = returned.reshape(expert_count * capacity, returned.shape[2])[slot_index].reshape(
        tok_count, TOPK, returned.shape[2]
    )
    combined = jnp.sum(picked.astype(jnp.float32) * gates[:, :, None], axis=1)
    expert_out = lax.psum_scatter(
        combined.astype(jnp.bfloat16), "head", scatter_dimension=1, tiled=True
    )
    return (attention, expert_out)


def solution(mesh):
    placed = (
        P("seq", "head"),
        P("seq", None),
        P("seq", None),
        P("head", None, None),
        P("head", None),
        P("seq", None),
        P(),
        P(),
        P("seq", None, "head"),
        P("seq", None, "head"),
        P("seq", "head", None),
        P(),
        P(),
        P("seq", None),
    )
    return jax.shard_map(
        on_device,
        mesh=mesh,
        in_specs=placed,
        out_specs=(P("seq", "head"), P("seq", "head")),
        check_vma=False,
    )
```

profile of v0, /device:TPU:1, one launch (start us, length us, event | category | flops | bytes accessed | tf_op | source)
XLA Modules:
  0.0 759.8 jit_solution(14834072606422764430)
XLA Ops:
  8.0 4.6 collective-permute-start
  20.7 1.2 fusion.10
  22.4 2.9 scatter_custom_fusion
  25.6 111.7 %all-gather.2.cloned.1.call-done = bf16[1024,576]{1,0:T(8,128)(2,1)} async-done(((bf16[16,576]{1,0:T(8,128)(2,1)}), bf16[1024,576]{1,0:T(8,128)(2,1)}) %all-gather.2.cloned.1.call-update) | async-done | bytes 1179664 | tf_op jit(solution)/shard_map/all_gather | solution.py:87
  137.3 2.1 fusion.26
  140.6 1.0 convolution_convert_fusion.1
  141.7 91.0 %all-reduce.3.cloned.1.call-done = bf16[64,2048]{1,0:T(8,128)(2,1)} async-done(((bf16[64,2048]{1,0:T(8,128)(2,1)}), bf16[64,2048]{1,0:T(8,128)(2,1)}) %all-reduce.3.cloned.1.call-update) | async-done | bytes 262160 | tf_op jit(solution)/shard_map/psum | solution.py:109
  232.7 1.1 multiply_reduce_fusion.1
  233.8 1.1 multiply_convert_fusion
  235.7 4.0 gather_fusion
  239.6 4.6 reshape.215
  244.3 207.3 %all_to_all.10 = bf16[64,9,2048]{2,1,0:T(8,128)(2,1)S(1)} all-to-all(bf16[64,9,2048]{2,1,0:T(8,128)(2,1)} %reshape.215), channel_id=1, replica_groups=mesh['seq'=64,'head'=8] {'seq'}, dimensions={0} | all-to-all | bytes 4718592 | tf_op jit(solution)/shard_map/all_to_all | solution.py:133
  451.5 1.9 copy-done.1
  453.5 3.5 convolution_bitcast_fusion.1
  456.9 5.6 convolution_convert_fusion
  462.5 3.5 copy.64
  466.0 8.3 %all-to-all-start.1 = ((bf16[64,9,2048]{2,1,0:T(8,128)(2,1)}), bf16[64,9,2048]{2,1,0:T(8,128)(2,1)}, u32[]{:S(2)}, u32[]{:S(2)}) async-start(bf16[64,9,2048]{2,1,0:T(8,128)(2,1)} %copy.64), calls=%async_computation.1 | async-start | bytes 8388608 | tf_op jit(solution)/shard_map/all_to_all | solution.py:142
  475.0 184.6 %all-to-all-done.1 = bf16[64,9,2048]{2,1,0:T(8,128)(2,1)} async-done(((bf16[64,9,2048]{2,1,0:T(8,128)(2,1)}), bf16[64,9,2048]{2,1,0:T(8,128)(2,1)}, u32[]{:S(2)}, u32[]{:S(2)}) %all-to-all-start.1) | async-done | bytes 2359328 | tf_op jit(solution)/shard_map/all_to_all | solution.py:142
  659.6 3.4 reshape.220
  663.0 3.1 gather_fusion.1
  666.1 3.9 reshape.221
  670.0 4.5 multiply_reduce_fusion
  674.5 1.4 dynamic-slice_convert_fusion
  675.9 77.4 %reduce-scatter.2.cloned.1.call-done = bf16[64,256]{1,0:T(8,128)(2,1)} async-done(((bf16[64,2048]{1,0:T(8,128)(2,1)}), bf16[64,256]{1,0:T(8,128)(2,1)}) %reduce-scatter.2.cloned.1.call-update) | async-done | bytes 32784 | tf_op jit(solution)/shard_map/reduce_scatter | solution.py:147
  (85 shorter events, 12.2 us)
Async XLA Ops:
  7.2 133.4 %copy-start = (bf16[256,2048]{1,0:T(8,128)(2,1)S(1)}, bf16[256,2048]{1,0:T(8,128)(2,1)}, u32[]{:S(2)}) copy-start(bf16[256,2048]{1,0:T(8,128)(2,1)} %param.18) | copy-start | bytes 3145732
  7.2 18.1 %copy-start.7 = (bf16[64,576]{1,0:T(8,128)(2,1)S(1)}, bf16[64,576]{1,0:T(8,128)(2,1)}, u32[]{:S(2)}) copy-start(bf16[64,576]{1,0:T(8,128)(2,1)} %param.15) | copy-start | bytes 221188
  7.2 130.1 %all-gather.2.cloned.1.call-start = ((), (), s32[]{:S(2)}) async-start(), calls=%async_computation.3 | async-start | bytes 1331200 | tf_op jit(solution)/shard_map/all_gather | solution.py:87
  7.9 224.7 %all-reduce.3.cloned.1.call-start = ((), (), s32[]{:S(2)}) async-start(), calls=%async_computation.4 | async-start | bytes 524288 | tf_op jit(solution)/shard_map/psum | solution.py:109
  8.0 17.3 %collective-permute-start = (bf16[64,576]{1,0:T(8,128)(2,1)}, bf16[64,576]{1,0:T(8,128)(2,1)S(1)}, u32[]{:S(2)}, u32[]{:S(2)}) collective-permute-start(bf16[64,576]{1,0:T(8,128)(2,1)} %param.15), channel_id=1, source_target_pairs={{0,8},{8,16},{16,24},{24,32},{32,40},{40,48},{48,56},{56,64},{64,7... | collective-permute-start | bytes 221192 | tf_op jit(solution)/shard_map/ppermute | solution.py:25
  137.3 2.4 copy-start.2
  139.4 1.0 copy-start.6
  139.7 93.0 %copy-start.3 = (bf16[64,2048]{1,0:T(8,128)(2,1)S(1)}, bf16[64,2048]{1,0:T(8,128)(2,1)}, u32[]{:S(2)}) copy-start(bf16[64,2048]{1,0:T(8,128)(2,1)} %param.19) | copy-start | bytes 786436
  234.9 0.7 copy-start.4
  244.3 209.2 %copy-start.9 = (bf16[1,2048,176]{1,2,0:T(8,128)(2,1)S(1)}, bf16[1,2048,176]{1,2,0:T(8,128)(2,1)}, u32[]{:S(2)}) copy-start(bf16[1,2048,176]{1,2,0:T(8,128)(2,1)} %param.22) | copy-start | bytes 2162692
  451.5 1.9 copy-start.1
  466.0 8.4 %copy-start.5 = (bf16[64,2048]{1,0:T(8,128)(2,1)S(1)}, bf16[64,2048]{1,0:T(8,128)(2,1)}, u32[]{:S(2)}) copy-start(bf16[64,2048]{1,0:T(8,128)(2,1)} %copy-done.4) | copy-start | bytes 786436
  466.0 8.4 %copy-start.10 = (bf16[2048,64]{0,1:T(8,128)(2,1)S(1)}, bf16[2048,64]{0,1:T(8,128)(2,1)}, u32[]{:S(2)}) copy-start(bf16[2048,64]{0,1:T(8,128)(2,1)} %param.21) | copy-start | bytes 786436
  466.0 8.6 %copy-start.8 = (s32[64,6]{0,1:T(8,128)S(1)}, s32[64,6]{0,1:T(8,128)}, u32[]{:S(2)}) copy-start(s32[64,6]{0,1:T(8,128)} %param.27) | copy-start | bytes 4612
  466.0 193.6 %all-to-all-start.1 = ((bf16[64,9,2048]{2,1,0:T(8,128)(2,1)}), bf16[64,9,2048]{2,1,0:T(8,128)(2,1)}, u32[]{:S(2)}, u32[]{:S(2)}) async-start(bf16[64,9,2048]{2,1,0:T(8,128)(2,1)} %copy.64), calls=%async_computation.1 | async-start | bytes 8388608 | tf_op jit(solution)/shard_map/all_to_all | solution.py:142
  474.3 279.0 %reduce-scatter.2.cloned.1.call-start = ((), (), s32[]{:S(2)}) async-start(), calls=%async_computation.5 | async-start | bytes 294912 | tf_op jit(solution)/shard_map/reduce_scatter | solution.py:147
Sparse Core Ops, SparseCore 0:
  10.1 127.1 all-gather.1
  141.8 90.8 all-reduce.2
  674.6 78.6 reduce-scatter.1
where the time goes:
time: 762 us; the launch traced here: 760 us
  waiting for transfers between devices  465 us (61%)
  blocking collectives  207 us (27%)
  local copies, waits for them, and re-layouts  33.7 us (4%)
  matrix products  14.5 us (2%)
  between operations  14.2 us (2%)
  starting transfers between devices  13 us (2%)
  other arithmetic  11.8 us (2%)
    all_to_all x1, blocking collectives, on_device(): lax.all_to_all(outgoing, 'seq', split_axis=0, concat_axis=0, tiled=True)  207 us
    all_to_all x1, waiting for transfers between devices, on_device(): lax.all_to_all(produced, 'seq', split_axis=0, concat_axis=0, tiled=True)  185 us
    all_gather x1, waiting for transfers between devices, on_device(): piece = lax.all_gather(prefix_latent, 'seq', axis=0, tiled=True)  112 us
    psum x1, waiting for transfers between devices, on_device(): lax.psum(partial_value.astype(jnp.bfloat16), 'head').astype(jnp.float32)  91 us
    reduce_scatter x1, waiting for transfers between devices, on_device(): lax.psum_scatter(combined.astype(jnp.bfloat16), 'head', scatter_dimension...  77.4 us
  transfers between devices with their start and end apart: 5, of which 4 were waited for; matrix products, arithmetic and copies ran while one was open for 2% of the time, Pallas kernels for 0%

commit v1 on v0

v1 whole, which is shorter than its diff:
```python
import math

import jax
import jax.numpy as jnp
from jax import lax
from jax.experimental import pallas as pl
from jax.experimental.pallas import tpu as pltpu
import numpy as np
from jax.sharding import PartitionSpec as P

D = 2048
NOPE = 128
ROPE = 64
VDIM = 128
LAT = 512
TOPK = 6
PRE_LEN = 512


score_scale = 1.0 / math.sqrt(192.0)
route_scale = 2.446
norm_eps = 1e-06


def request_info(lengths, group_map, position):
    request_ends = jnp.cumsum(lengths)
    request_starts = request_ends - lengths
    request_index = jnp.sum((request_ends[None, :] <= position[:, None]).astype(jnp.int32), axis=1)
    member = (
        request_index[:, None] == jnp.arange(lengths.shape[0], dtype=jnp.int32)[None, :]
    ).astype(jnp.int32)
    first_token = jnp.sum(member * request_starts[None, :], axis=1)
    token_group = jnp.sum(member * group_map[None, :], axis=1)
    return (first_token, token_group)


N_HEAD = 8
N_Z = 16
N_MATE = 4
CAP = 9
TOK = 64
COLS = D // N_HEAD
SLOTS = N_Z * N_MATE * CAP
MATE_ROWS = N_Z * CAP
Z_ROWS = N_MATE * CAP
Z_PAD = 48
PADDED = N_Z * Z_PAD
MESH = pl.DeviceIdType.MESH


def remote(src, dst, send_sem, recv_sem, device):
    return pltpu.make_async_remote_copy(
        src_ref=src,
        dst_ref=dst,
        send_sem=send_sem,
        recv_sem=recv_sem,
        device_id=device,
        device_id_type=MESH,
    )


def gather_kernel(
    prefix_ref, suffix_ref, keys_ref, local_sem, near_send, near_recv,
    seq_send, seq_recv, head_send, head_recv, core_send, core_recv,
):
    seq = lax.axis_index("seq")
    head = lax.axis_index("head")
    core = lax.rem(seq, 2)
    chip = seq // 2
    z = chip // 2
    lane = lax.rem(chip, 2)
    after = lax.rem(seq + 1, 64)
    before = lax.rem(seq + 63, 64)
    partner = seq + 1 - 2 * core

    barrier = pltpu.get_barrier_semaphore()

    def greet(n, carry):
        other = lax.rem(chip + n, 32) * 2 + core
        pl.semaphore_signal(barrier, inc=1, device_id=(other, head), device_id_type=MESH)
        return carry

    lax.fori_loop(1, 32, greet, 0)
    for n in range(1, N_HEAD):
        pl.semaphore_signal(
            barrier, inc=1, device_id=(seq, lax.rem(head + n, N_HEAD)), device_id_type=MESH
        )
    for other in (partner, after, before):
        pl.semaphore_signal(barrier, inc=1, device_id=(other, head), device_id_type=MESH)
    own_copy = pltpu.make_async_copy(suffix_ref, keys_ref.at[pl.ds(1088, 64)], local_sem.at[0])
    own_copy.start()
    pl.semaphore_wait(barrier, 31 + 7 + 3)

    near = remote(
        suffix_ref, keys_ref.at[pl.ds(1024, 64)], near_send.at[0], near_recv.at[0], (after, head)
    )
    near.start()

    base = core * 512
    group_base = base + head * 64
    mine = lax.rem(z, 8) == head
    slot = (z // 8) * 2 + lane
    place = pl.multiple_of(base + lax.rem(z, 8) * 64 + slot * 16, 16)

    def to_chip(n):
        other = lax.rem(chip + n, 32) * 2 + core
        return remote(
            prefix_ref, keys_ref.at[pl.ds(place, 16)], seq_send.at[n], seq_recv.at[slot],
            (other, head),
        )

    @pl.when(mine)
    def _():
        def send(n, carry):
            to_chip(n).start()
            return carry

        lax.fori_loop(1, 32, send, 0)
        keep = pltpu.make_async_copy(prefix_ref, keys_ref.at[pl.ds(place, 16)], local_sem.at[1])
        keep.start()
        keep.wait()

    for k in range(4):
        origin = (head + 8 * (k // 2)) * 2 + (k % 2)
        from_row = pl.multiple_of(group_base + k * 16, 16)

        @pl.when(origin != chip)
        def _():
            remote(
                prefix_ref, keys_ref.at[pl.ds(from_row, 16)], seq_send.at[0], seq_recv.at[k],
                (partner, head),
            ).wait_recv()

    def rows_of(which, owner):
        return keys_ref.at[pl.ds(pl.multiple_of(which * 512 + owner * 64, 64), 64)]

    for n in range(1, N_HEAD):
        remote(
            rows_of(core, head), rows_of(core, head), head_send.at[n], head_recv.at[head],
            (seq, lax.rem(head + n, N_HEAD)),
        ).start()
    for n in range(N_HEAD):
        owner = lax.rem(head + n, N_HEAD)
        if n:
            remote(
                rows_of(core, owner), rows_of(core, owner), head_send.at[n], head_recv.at[owner],
                (seq, owner),
            ).wait_recv()
        remote(
            rows_of(core, owner), rows_of(core, owner), core_send.at[owner], core_recv.at[owner],
            (partner, head),
        ).start()
    for owner in range(N_HEAD):
        remote(
            rows_of(core, owner), rows_of(1 - core, owner), core_send.at[owner],
            core_recv.at[owner], (partner, head),
        ).wait()

    for n in range(1, N_HEAD):
        remote(
            rows_of(core, head), rows_of(core, head), head_send.at[n], head_recv.at[head],
            (seq, lax.rem(head + n, N_HEAD)),
        ).wait_send()

    @pl.when(mine)
    def _():
        def drain(n, carry):
            to_chip(n).wait_send()
            return carry

        lax.fori_loop(1, 32, drain, 0)

    near.wait()
    own_copy.wait()


def gather_keys(prefix_latent, suffix_latent):
    dma = pltpu.SemaphoreType.DMA
    vmem = pl.BlockSpec(memory_space=pltpu.VMEM)
    return pl.pallas_call(
        gather_kernel,
        out_shape=jax.ShapeDtypeStruct((1152, LAT + ROPE), jnp.bfloat16),
        in_specs=[vmem] * 2,
        out_specs=vmem,
        scratch_shapes=[
            dma((2,)), dma((1,)), dma((1,)), dma((32,)), dma((4,)),
            dma((8,)), dma((8,)), dma((8,)), dma((8,)),
        ],
        compiler_params=pltpu.CompilerParams(collective_id=0, has_side_effects=True),
    )(prefix_latent, suffix_latent)


def slot_tables():
    slot = np.arange(SLOTS)
    mate, z, rank = slot // MATE_ROWS, slot % MATE_ROWS // CAP, slot % CAP
    expert = z * N_MATE + mate
    row = np.arange(PADDED)
    q = row % Z_PAD
    to_z = np.where(q < Z_ROWS, q // CAP * MATE_ROWS + row // Z_PAD * CAP + q % CAP, -1)
    unpad = slot + (Z_PAD - Z_ROWS) * (slot // Z_ROWS)
    return [v.astype(np.int32) for v in (expert, rank, to_z, unpad)]


def picks(column, width):
    wide = lax.broadcasted_iota(jnp.int32, (column.shape[0], width), 1)
    return jnp.where(wide == column, 1.0, 0.0).astype(jnp.bfloat16)


def picked_by(row, height):
    tall = lax.broadcasted_iota(jnp.int32, (height, row.shape[1]), 0)
    return jnp.where(tall == row, 1.0, 0.0).astype(jnp.bfloat16)


def matmul(a, b):
    return jnp.dot(a, b, preferred_element_type=jnp.float32)


def experts_kernel(
    partial_ref, residual_ref, gain_ref, router_ref, ids_ref,
    expert_col, rank_col, to_z_col, unpad_col,
    expert_row, rank_row, to_z_row, unpad_row,
    gate_ref, up_ref, down_ref,
    attention_ref, out_ref,
    sum_buf, sq_out, sq_buf, lg_out, lg_buf, slots, mates, z_out, z_in, x_buf,
    gate_acc, up_acc, inner_ref, down_out, down_in, back_out, back_in, home_out, home_in,
    sum_send, sum_recv, sq_send, sq_recv, lg_send, lg_recv, mate_send, mate_recv,
    z_send, z_recv, x_send, x_recv, down_send, down_recv, back_send, back_recv,
    home_send, home_recv,
):
    seq = lax.axis_index("seq")
    head = lax.axis_index("head")
    z = seq // N_MATE
    mate = lax.rem(seq, N_MATE)

    def head_peer(n):
        return lax.rem(head + n, N_HEAD)

    def mate_peer(n):
        return lax.rem(mate + n, N_MATE)

    def z_peer(n):
        return lax.rem(z + n, N_Z)

    barrier = pltpu.get_barrier_semaphore()

    def greet(n, carry):
        pl.semaphore_signal(
            barrier, inc=1, device_id=(z_peer(n) * N_MATE + mate, head), device_id_type=MESH
        )
        return carry

    lax.fori_loop(1, N_Z, greet, 0)
    for n in range(1, N_HEAD):
        pl.semaphore_signal(barrier, inc=1, device_id=(seq, head_peer(n)), device_id_type=MESH)
    for n in range(1, N_MATE):
        pl.semaphore_signal(
            barrier, inc=1, device_id=(z * N_MATE + mate_peer(n), head), device_id_type=MESH
        )

    lanes = lax.broadcasted_iota(jnp.int32, (TOK, 64), 1)
    member = jnp.zeros((TOK, 64), jnp.float32)
    for k in range(TOPK):
        member = member + jnp.where(ids_ref[:, k : k + 1] == lanes, 1.0, 0.0)
    below = jnp.where(lax.broadcasted_iota(jnp.int32, (TOK, 64), 0) > lanes, 1.0, 0.0)
    rank = matmul(below.astype(jnp.bfloat16), member.astype(jnp.bfloat16))
    rank = jnp.where(member > 0.5, rank, -1.0).astype(jnp.bfloat16)
    slot_rank = lax.dot_general(
        picks(expert_col[...], 64), rank, (((1,), (1,)), ((), ())),
        preferred_element_type=jnp.float32,
    )
    takes = jnp.where(slot_rank == rank_col[...].astype(jnp.float32), 1.0, 0.0).astype(jnp.bfloat16)

    pl.semaphore_wait(barrier, N_Z - 1 + N_HEAD - 1 + N_MATE - 1)

    def cols(owner):
        return pl.ds(pl.multiple_of(owner * COLS, COLS), COLS)

    def sum_copy(n):
        return remote(
            partial_ref.at[:, cols(head_peer(n))], sum_buf.at[head], sum_send.at[n],
            sum_recv.at[head], (seq, head_peer(n)),
        )

    def take(buf, send, recv, n):
        owner = head_peer(n)
        remote(buf.at[owner], buf.at[owner], send.at[n], recv.at[owner], (seq, owner)).wait_recv()

    for n in range(1, N_HEAD):
        sum_copy(n).start()
    attention = partial_ref[:, cols(head)].astype(jnp.float32)
    for n in range(1, N_HEAD):
        take(sum_buf, sum_send, sum_recv, n)
        attention = attention + sum_buf[head_peer(n)].astype(jnp.float32)
    attention_ref[...] = attention.astype(jnp.bfloat16)
    hidden = residual_ref[:, cols(head)].astype(jnp.float32) + attention
    square = jnp.sum(hidden * hidden, axis=1, keepdims=True)
    square = jnp.concatenate(
        [jnp.broadcast_to(square, (TOK, 128)), jnp.zeros((128 - TOK, 128), jnp.float32)], axis=0
    )
    square = jnp.transpose(square)[:8]
    sq_out[...] = square

    def sq_copy(n):
        return remote(
            sq_out, sq_buf.at[head], sq_send.at[n], sq_recv.at[head], (seq, head_peer(n))
        )

    for n in range(1, N_HEAD):
        sq_copy(n).start()
    for n in range(1, N_HEAD):
        take(sq_buf, sq_send, sq_recv, n)
        square = square + sq_buf[head_peer(n)]
    mean_square = jnp.transpose(jnp.broadcast_to(square[:1], (128, 128)))[:TOK, :1] * (1.0 / D)
    gain = gain_ref[:, cols(head)].astype(jnp.float32)
    normed = (hidden * lax.rsqrt(mean_square + norm_eps) * gain).astype(jnp.bfloat16)

    slots[...] = matmul(takes, normed).astype(jnp.bfloat16)

    def rows(owner):
        return pl.ds(pl.multiple_of(owner * MATE_ROWS, MATE_ROWS), MATE_ROWS)

    def mate_copy(src, dst, send, recv, n):
        owner = mate_peer(n)
        return remote(
            src.at[rows(owner)], dst.at[rows(mate)], send.at[n], recv.at[mate],
            (z * N_MATE + owner, head),
        )

    def mate_take(dst, send, recv, n):
        owner = mate_peer(n)
        remote(
            dst.at[rows(owner)], dst.at[rows(owner)], send.at[n], recv.at[owner],
            (z * N_MATE + owner, head),
        ).wait_recv()

    for n in range(1, N_MATE):
        mate_copy(slots, mates, mate_send, mate_recv, n).start()
    mates[rows(mate), :] = slots[rows(mate), :]

    lg_out[...] = matmul(normed, router_ref[cols(head), :])

    def lg_copy(n):
        return remote(
            lg_out, lg_buf.at[head], lg_send.at[n], lg_recv.at[head], (seq, head_peer(n))
        )

    for n in range(1, N_MATE):
        mate_take(mates, mate_send, mate_recv, n)
    z_out[...] = matmul(picks(to_z_col[...], SLOTS), mates[...]).astype(jnp.bfloat16)

    def z_rows(owner):
        return pl.ds(pl.multiple_of(owner * Z_PAD, Z_PAD), Z_PAD)

    def z_exchange(src, dst, send, recv):
        def copy(n):
            owner = z_peer(n)
            return remote(
                src.at[z_rows(owner)], dst.at[z_rows(z)], send.at[n], recv.at[z],
                (owner * N_MATE + mate, head),
            )

        def start(n, carry):
            copy(n).start()
            return carry

        def arrive(n, carry):
            owner = z_peer(n)
            remote(
                dst.at[z_rows(owner)], dst.at[z_rows(owner)], send.at[n], recv.at[owner],
                (owner * N_MATE + mate, head),
            ).wait_recv()
            return carry

        def drain(n, carry):
            copy(n).wait_send()
            return carry

        lax.fori_loop(1, N_Z, start, 0)
        dst[z_rows(z), :] = src[z_rows(z), :]
        return arrive, drain

    arrive, drain_z = z_exchange(z_out, z_in, z_send, z_recv)
    for n in range(1, N_HEAD):
        lg_copy(n).start()
    lax.fori_loop(1, N_Z, arrive, 0)
    x_buf[head] = matmul(picks(unpad_col[...], PADDED), z_in[...]).astype(jnp.bfloat16)

    def x_copy(n):
        return remote(
            x_buf.at[head], x_buf.at[head], x_send.at[n], x_recv.at[head], (seq, head_peer(n))
        )

    for n in range(1, N_HEAD):
        x_copy(n).start()
    gate_acc[...] = matmul(x_buf[head], gate_ref[cols(head), :])
    up_acc[...] = matmul(x_buf[head], up_ref[cols(head), :])

    def accumulate(n, carry):
        take(x_buf, x_send, x_recv, n)
        owner = head_peer(n)
        gate_acc[...] += matmul(x_buf[owner], gate_ref[cols(owner), :])
        up_acc[...] += matmul(x_buf[owner], up_ref[cols(owner), :])
        return carry

    lax.fori_loop(1, N_HEAD, accumulate, 0)
    gate = gate_acc[...]
    inner_ref[...] = (gate / (1.0 + jnp.exp(-gate)) * up_acc[...]).astype(jnp.bfloat16)

    def down_copy(n):
        owner = head_peer(n)
        return remote(
            down_out.at[owner], down_in.at[head], down_send.at[n], down_recv.at[head], (seq, owner)
        )

    def project(n, carry):
        owner = head_peer(n)
        down_out[owner] = matmul(inner_ref[...], down_ref[:, cols(owner)]).astype(jnp.bfloat16)
        down_copy(n).start()
        return carry

    lax.fori_loop(1, N_HEAD, project, 0)
    own_part = matmul(inner_ref[...], down_ref[:, cols(head)]).astype(jnp.bfloat16)
    gate_acc2 = own_part.astype(jnp.float32)

    logits = lg_out[...]
    for n in range(1, N_HEAD):
        take(lg_buf, lg_send, lg_recv, n)
        logits = logits + lg_buf[head_peer(n)]
    chosen = jnp.where(member > 0.5, 1.0 / (1.0 + jnp.exp(-logits)), 0.0)
    gates = chosen / jnp.sum(chosen, axis=1, keepdims=True) * route_scale
    by_expert = picked_by(expert_row[...], 64)
    gates_high = gates.astype(jnp.bfloat16)
    gates_low = (gates - gates_high.astype(jnp.float32)).astype(jnp.bfloat16)
    given = matmul(rank, by_expert) == rank_row[...].astype(jnp.float32)
    mix_high = jnp.where(given, matmul(gates_high, by_expert), 0.0).astype(jnp.bfloat16)
    mix_low = jnp.where(given, matmul(gates_low, by_expert), 0.0).astype(jnp.bfloat16)

    total = gate_acc2
    for n in range(1, N_HEAD):
        take(down_in, down_send, down_recv, n)
        total = total + down_in[head_peer(n)].astype(jnp.float32)
    summed = total.astype(jnp.bfloat16)
    back_out[...] = matmul(picked_by(unpad_row[...], PADDED), summed).astype(jnp.bfloat16)
    arrive, drain_back = z_exchange(back_out, back_in, back_send, back_recv)
    lax.fori_loop(1, N_Z, arrive, 0)
    home_out[...] = matmul(picked_by(to_z_row[...], SLOTS), back_in[...]).astype(jnp.bfloat16)
    for n in range(1, N_MATE):
        mate_copy(home_out, home_in, home_send, home_recv, n).start()
    home_in[rows(mate), :] = home_out[rows(mate), :]
    for n in range(1, N_MATE):
        mate_take(home_in, home_send, home_recv, n)
    out_ref[...] = (matmul(mix_high, home_in[...]) + matmul(mix_low, home_in[...])).astype(
        jnp.bfloat16
    )

    for n in range(1, N_HEAD):
        sum_copy(n).wait_send()
        sq_copy(n).wait_send()
        lg_copy(n).wait_send()
        x_copy(n).wait_send()
        down_copy(n).wait_send()
    for n in range(1, N_MATE):
        mate_copy(slots, mates, mate_send, mate_recv, n).wait_send()
        mate_copy(home_out, home_in, home_send, home_recv, n).wait_send()
    lax.fori_loop(1, N_Z, drain_z, 0)
    lax.fori_loop(1, N_Z, drain_back, 0)


def route_and_mix(partial, residual, norm_gain, router, expert_ids, w_gate, w_up, w_down):
    dma = pltpu.SemaphoreType.DMA
    vmem = pl.BlockSpec(memory_space=pltpu.VMEM)
    low, wide = jnp.bfloat16, jnp.float32
    hidden = w_gate.shape[1]
    tables = slot_tables()
    columns = [jnp.asarray(v[:, None]) for v in tables]
    across = [jnp.asarray(v[None, :]) for v in tables]
    out = jax.ShapeDtypeStruct((TOK, COLS), low)
    return pl.pallas_call(
        experts_kernel,
        out_shape=(out, out),
        in_specs=[vmem] * 16,
        out_specs=(vmem, vmem),
        scratch_shapes=[
            pltpu.VMEM((N_HEAD, TOK, COLS), low),
            pltpu.VMEM((8, 128), wide),
            pltpu.VMEM((N_HEAD, 8, 128), wide),
            pltpu.VMEM((TOK, 64), wide),
            pltpu.VMEM((N_HEAD, TOK, 64), wide),
            pltpu.VMEM((SLOTS, COLS), low),
            pltpu.VMEM((SLOTS, COLS), low),
            pltpu.VMEM((PADDED, COLS), low),
            pltpu.VMEM((PADDED, COLS), low),
            pltpu.VMEM((N_HEAD, SLOTS, COLS), low),
            pltpu.VMEM((SLOTS, hidden), wide),
            pltpu.VMEM((SLOTS, hidden), wide),
            pltpu.VMEM((SLOTS, hidden), low),
            pltpu.VMEM((N_HEAD, SLOTS, COLS), low),
            pltpu.VMEM((N_HEAD, SLOTS, COLS), low),
            pltpu.VMEM((PADDED, COLS), low),
            pltpu.VMEM((PADDED, COLS), low),
            pltpu.VMEM((SLOTS, COLS), low),
            pltpu.VMEM((SLOTS, COLS), low),
        ]
        + [dma((N_HEAD,))] * 6
        + [dma((N_MATE,))] * 2
        + [dma((N_Z,))] * 2
        + [dma((N_HEAD,))] * 4
        + [dma((N_Z,))] * 2
        + [dma((N_MATE,))] * 2,
        compiler_params=pltpu.CompilerParams(
            collective_id=1, has_side_effects=True, vmem_limit_bytes=48 * 1024 * 1024
        ),
    )(partial, residual, norm_gain, router, expert_ids, *columns, *across, w_gate, w_up, w_down)


def on_device(
    queries,
    suffix_latent,
    prefix_latent,
    kv_up,
    w_out,
    residual,
    norm_gain,
    router,
    w_gate,
    w_up,
    w_down,
    lengths,
    group_map,
    expert_ids,
):
    tok_count = queries.shape[0]
    head_local = kv_up.shape[0]
    seq_index = lax.axis_index("seq")
    first_row = seq_index * tok_count
    position = first_row + jnp.arange(tok_count, dtype=jnp.int32)
    first_token, token_group = request_info(lengths, group_map, position)
    query_block = queries.reshape(tok_count, head_local, NOPE + ROPE)
    absorbed = jnp.einsum(
        "thn,hln->thl",
        query_block[:, :, :NOPE],
        kv_up[:, :, :NOPE],
        preferred_element_type=jnp.float32,
    ).astype(jnp.bfloat16)
    joined = jnp.concatenate([absorbed, query_block[:, :, NOPE:]], axis=2).reshape(
        tok_count * head_local, LAT + ROPE
    )
    keys = gather_keys(prefix_latent, suffix_latent)
    column = jnp.arange(keys.shape[0], dtype=jnp.int32)
    near_pos = (first_row - tok_count + column - 2 * PRE_LEN)[None, :]
    near_seen = (near_pos >= first_token[:, None]) & (near_pos <= position[:, None])
    far_seen = (column[None, :] // 32) % 2 == token_group[:, None]
    seen = jnp.where(column[None, :] < 2 * PRE_LEN, far_seen, near_seen)
    seen = jnp.repeat(seen, head_local, axis=0)
    scores = jnp.dot(joined, keys.T, preferred_element_type=jnp.float32) * score_scale
    row_max = jnp.max(jnp.where(seen, scores, -jnp.inf), axis=1, keepdims=True)
    weights = jnp.where(seen, jnp.exp(scores - row_max), 0.0)
    total = jnp.sum(weights, axis=1, keepdims=True)
    weighted = jnp.dot(
        weights.astype(jnp.bfloat16), keys[:, :LAT], preferred_element_type=jnp.float32
    )
    mixed = (weighted / total).astype(jnp.bfloat16).reshape(tok_count, head_local, LAT)
    heads_out = jnp.einsum(
        "thl,hlv->thv", mixed, kv_up[:, :, NOPE:], preferred_element_type=jnp.float32
    ).astype(jnp.bfloat16)
    partial_value = jnp.dot(
        heads_out.reshape(tok_count, head_local * VDIM), w_out, preferred_element_type=jnp.float32
    )
    return route_and_mix(
        partial_value.astype(jnp.bfloat16),
        residual,
        norm_gain.reshape(1, D),
        router,
        expert_ids,
        w_gate[0],
        w_up[0],
        w_down[0],
    )


def solution(mesh):
    placed = (
        P("seq", "head"),
        P("seq", None),
        P("seq", None),
        P("head", None, None),
        P("head", None),
        P("seq", None),
        P(),
        P(),
        P("seq", None, "head"),
        P("seq", None, "head"),
        P("seq", "head", None),
        P(),
        P(),
        P("seq", None),
    )
    return jax.shard_map(
        on_device,
        mesh=mesh,
        in_specs=placed,
        out_specs=(P("seq", "head"), P("seq", "head")),
        check_vma=False,
    )
```

time: 762 us -> 205 us (0.27)
  the two profiles are of different devices: /device:TPU:1 before, /device:TPU:93 now
where the time goes in v1:
time: 205 us
  Pallas kernels  181 us (88%)
  local copies, waits for them, and re-layouts  15.6 us (8%)
  matrix products  4.17 us (2%)
  other arithmetic  2.43 us (1%)
    pallas_call x1, Pallas kernels, route_and_mix(): pl.pallas_call(experts_kernel, out_shape=(out, out), in_specs=[vmem] * 16...  146 us
    pallas_call x1, Pallas kernels, gather_keys(): pl.pallas_call(gather_kernel, out_shape=jax.ShapeDtypeStruct((1152, LAT +...  35.7 us
    unnamed x41, local copies, waits for them, and re-layouts  12.8 us

profile of v1, /device:TPU:93, one launch (start us, length us, event | category | flops | bytes accessed | tf_op | source)
XLA Modules:
  0.0 204.6 jit_solution(17251243322108983021)
XLA Ops:
  0.7 0.8 copy.40
  2.0 0.7 sub.27
  2.6 0.8 select_reduce_fusion.2
  3.9 0.4 reshape.122
  4.3 0.9 reshape.123
  5.3 1.2 fusion.8
  6.8 35.7 %shard_map.221 = bf16[1152,576]{1,0:T(8,128)(2,1)} custom-call(bf16[16,576]{1,0:T(8,128)(2,1)} %prefix_ref.1, bf16[64,576]{1,0:T(8,128)(2,1)} %suffix_ref.1), custom_call_target="tpu_custom_call" | custom-call | tf_op jit(solution)/shard_map/pallas_call | solution.py:180
  42.5 2.1 %select_reduce_fusion = (f32[128]{0:T(128)S(1)}, f32[128,1152]{1,0:T(8,128)S(1)}) fusion(pred[128,1152]{1,0:T(32,128)(4,1)S(1)} %reshape.122, bf16[128,576]{1,0:T(8,128)(2,1)S(1)} %reshape.124, bf16[1152,576]{1,0:T(8,128)(2,1)} %shard_map.221), kind=kOutput, calls=%fused_computation.11 | convolution fusion | flops 170311552 | bytes 2212352 | tf_op jit(solution)/shard_map/dot_general | solution.py:555
  44.9 0.4 fusion.5
  45.4 0.5 copy-done.14
  46.2 0.3 convolution_convert_fusion.partial_ref
  46.5 0.5 copy.46
  47.1 1.4 copy.47
  48.5 1.9 copy.48.router_ref
  50.6 1.0 copy-done.1
  51.7 1.1 copy-done.2
  52.8 1.0 copy-done.3
  53.8 1.0 copy-done.4
  54.7 1.0 copy-done.5
  55.7 1.0 copy-done.6
  56.7 0.9 copy-done.7
  57.6 145.8 %shard_map.222 = (bf16[64,256]{1,0:T(8,128)(2,1)S(1)}, bf16[64,256]{1,0:T(8,128)(2,1)S(1)}) custom-call(bf16[64,2048]{1,0:T(8,128)(2,1)S(1)} %convolution_convert_fusion.partial_ref, bf16[64,2048]{1,0:T(8,128)(2,1)S(1)} %copy-done.7, bf16[1,2048]{1,0:T(2,128)(2,1)S(1)} %reshape.127.gain_ref, bf16[2048,64]{1,0:T(8,128)(2,1)S(1)} %copy-done.1, ...), custom_call_target="tpu_custom_call" | custom-call | tf_op jit(solution)/shard_map/pallas_call | solution.py:478
  203.4 0.6 copy.66
  204.0 0.6 copy.67
  (45 shorter events, 2.0 us)
Async XLA Ops:
  0.6 45.5 %copy-start = (bf16[256,2048]{1,0:T(8,128)(2,1)S(1)}, bf16[256,2048]{1,0:T(8,128)(2,1)}, u32[]{:S(2)}) copy-start(bf16[256,2048]{1,0:T(8,128)(2,1)} %param.26) | copy-start | bytes 3145732
  42.5 2.4 %copy-start.12 = (bf16[1152,576]{1,0:T(8,128)(2,1)S(1)}, bf16[1152,576]{1,0:T(8,128)(2,1)}, u32[]{:S(2)}) copy-start(bf16[1152,576]{1,0:T(8,128)(2,1)} %shard_map.221) | copy-start | bytes 3981316
  44.9 1.0 copy-start.14
  45.4 1.1 copy-start.13
  47.0 3.5 %copy-start.15 = (s32[64,6]{0,1:T(8,128)S(1)}, s32[64,6]{0,1:T(8,128)}, u32[]{:S(2)}) copy-start(s32[64,6]{0,1:T(8,128)} %param.35) | copy-start | bytes 4612
  47.0 3.6 %copy-start.16 = (bf16[2048]{0:T(1024)(128)(2,1)S(1)}, bf16[2048]{0:T(1024)(128)(2,1)}, u32[]{:S(2)}) copy-start(bf16[2048]{0:T(1024)(128)(2,1)} %param.28) | copy-start | bytes 12292
  47.0 3.6 %copy-start.8 = (s32[1,768]{1,0:T(1,128)S(1)}, s32[1,768]{1,0:T(1,128)}, u32[]{:S(2)}) copy-start(s32[1,768]{1,0:T(1,128)} %constant.80.clone.to_z_row) | copy-start | bytes 9220
  47.0 3.6 %copy-start.9 = (s32[1,576]{1,0:T(1,128)S(1)}, s32[1,576]{1,0:T(1,128)}, u32[]{:S(2)}) copy-start(s32[1,576]{1,0:T(1,128)} %constant.78.clone.expert_row) | copy-start | bytes 6916
  47.0 3.6 %copy-start.10 = (s32[1,576]{1,0:T(1,128)S(1)}, s32[1,576]{1,0:T(1,128)}, u32[]{:S(2)}) copy-start(s32[1,576]{1,0:T(1,128)} %constant.79.clone.rank_row) | copy-start | bytes 6916
  47.1 3.6 %copy-start.11 = (s32[1,576]{1,0:T(1,128)S(1)}, s32[1,576]{1,0:T(1,128)}, u32[]{:S(2)}) copy-start(s32[1,576]{1,0:T(1,128)} %constant.81.clone.unpad_row) | copy-start | bytes 6916
  50.6 1.0 copy-start.1
  51.7 1.1 copy-start.2
  52.8 1.0 copy-start.3
  53.8 1.0 copy-start.4
  54.7 1.0 copy-start.5
  55.7 1.0 copy-start.6
  56.7 0.9 copy-start.7
